TPU v7x, 32 devices: a whole 2x2x4 slice. The times are simulated.
32 devices in a mesh: dp: 16 (over z, y, core), mp: 2 (over x).
Axes of the slice: x: 2, y: 2, z: 4, core: 2. Of those that a mesh axis runs over, the one named last changes fastest.
Arguments:
- hidden_in: bfloat16 [8192, 4096], P('dp'), may hold values from -1.5 to 1.5
- w_query: bfloat16 [4096, 4096], P('dp', 'mp'), may hold values from -1 to 1
- w_key: bfloat16 [4096, 1024], P('dp', 'mp'), may hold values from -24 to 24
- w_value: bfloat16 [4096, 1024], P('dp', 'mp'), may hold values from -1 to 1
- w_out: bfloat16 [4096, 4096], P('dp', 'mp'), may hold values from -1 to 1
- value_weight: float32 [4096], P('mp'), may hold values from -0.09375 to 0.09375
- rewards: float32 [8192], P('dp'), may hold values from -0.6 to 0.6
- old_values: float32 [8192], P('dp'), may hold values from -6 to 6
- lengths: int32 [64], replicated, may hold values from 1 to 2048, 8192 in all
- terminal: int32 [64], replicated, may hold values 0 or 1
Outputs:
- value: float32 [8192], P('dp')
- advantage: float32 [8192], P('dp')
- value_loss: float32 [], replicated
All inputs are finite; a program needn't handle non-finite values.
Results may differ from a plain program's by a relative error of at most 0.012.
The roundings to bfloat16 on the way count: a program that leaves them out, or rounds other values in their place, can miss the bound.
Values may be sent and summed in bfloat16 or wider, within the bound.
No kernel may reach another device: no remote copies, remote signals or barrier semaphores. Data moves between devices by JAX's collectives and lax.ppermute only.
A program may use at most 128 MiB of HBM per device.

v0:
```python
import jax
import jax.numpy as jnp
from jax import lax
from jax.sharding import PartitionSpec as P

HEAD = 128
discount = 0.999
trace_decay = 0.997
clip_range = 0.2
epsilon = 1e-05
rope_base = 500000.0


def from_behind(array, axis, by):
    size = lax.axis_size(axis)
    pairs = [(i, i + by) for i in range(size) if 0 <= i + by < size]
    return lax.ppermute(array, axis, pairs)


def carried_in(part, axis, combine, identity):
    count = lax.axis_size(axis)
    place = lax.axis_index(axis)
    ahead = count - 1 - place
    gathered = jax.tree.map(lambda a: lax.all_gather(a, axis), part)
    state = jax.tree.map(lambda a, e: jnp.zeros_like(a) + jnp.asarray(e, a.dtype), part, identity)

    def one(hop, state):
        source = count - 1 - hop
        return combine(
            state, jax.tree.map(lambda a: lax.dynamic_index_in_dim(a, source, 0, False), gathered)
        )

    return lax.fori_loop(0, ahead, one, state)


def rotate(states, positions):
    half = HEAD // 2
    freq = rope_base ** (-jnp.arange(half, dtype=jnp.float32) * 2.0 / HEAD)
    angles = positions[:, None] * freq[None, :]
    cosine = jnp.cos(angles)[:, None, :]
    sine = jnp.sin(angles)[:, None, :]
    first = states[..., :half]
    second = states[..., half:]
    return jnp.concatenate([first * cosine - second * sine, second * cosine + first * sine], -1)


def body(
    hidden_in, w_query, w_key, w_value, w_out, value_weight, rewards, old_values, lengths, terminal
):
    rows = hidden_in.shape[0]
    width = hidden_in.shape[1]
    states = hidden_in.astype(jnp.float32)
    normed = (states * lax.rsqrt(jnp.mean(states * states, 1, keepdims=True) + epsilon)).astype(
        jnp.bfloat16
    )
    pieces = (
        lax.all_gather(w_query, "dp", axis=0, tiled=True),
        lax.all_gather(w_key, "dp", axis=0, tiled=True),
        lax.all_gather(w_value, "dp", axis=0, tiled=True),
        lax.all_gather(w_out, "dp", axis=0, tiled=True),
    )
    add_pieces = pieces[:3]
    summed = tuple(
        (jnp.dot(normed, piece, preferred_element_type=jnp.float32) for piece in add_pieces)
    )
    stored = pieces[3]
    query_sum, key_sum, value_sum, whole_out = summed + (stored,)
    position_ids = lax.axis_index("dp") * rows + jnp.arange(rows, dtype=jnp.int32)
    positions = position_ids.astype(jnp.float32)
    local_heads = w_query.shape[1] // HEAD
    local_kv = w_key.shape[1] // HEAD
    group = local_heads // local_kv
    query = rotate(query_sum.reshape(rows, local_heads, HEAD), positions).astype(jnp.bfloat16)
    key = rotate(key_sum.reshape(rows, local_kv, HEAD), positions).astype(jnp.bfloat16)
    values_proj = value_sum.astype(jnp.bfloat16).reshape(rows, local_kv, HEAD)
    ends = jnp.cumsum(lengths)
    matches = ends[None, :] - 1 == position_ids[:, None]
    finished = jnp.any(matches, 1).astype(jnp.float32)
    stopped = jnp.sum(jnp.where(matches, terminal[None, :], 0), 1).astype(jnp.float32)
    episode = jnp.sum((ends[None, :] <= position_ids[:, None]).astype(jnp.int32), 1)
    order = jnp.arange(rows, dtype=jnp.int32)
    same_episode = episode[None, :] == episode[:, None]
    allowed = (order[None, :] <= order[:, None]) & same_episode
    scores = jnp.einsum(
        "tkgd,skd->kgts",
        query.reshape(rows, local_kv, group, HEAD),
        key,
        preferred_element_type=jnp.float32,
    ) * (1.0 / HEAD**0.5)
    masked = jnp.where(allowed[None, None], scores, -1e30)
    largest = jnp.max(masked, -1, keepdims=True)
    expon = jnp.where(allowed[None, None], jnp.exp(masked - largest), 0.0)
    probs = (expon / jnp.sum(expon, -1, keepdims=True)).astype(jnp.bfloat16)
    output = jnp.einsum("kgts,skd->tkgd", probs, values_proj, preferred_element_type=jnp.float32)
    attended = output.astype(jnp.bfloat16).reshape(rows, local_heads * HEAD)
    all_heads = lax.all_gather(attended, "mp", axis=1, tiled=True)
    projected = jnp.dot(all_heads, whole_out, preferred_element_type=jnp.float32)
    feature_count = w_out.shape[1]
    own_states = lax.dynamic_slice_in_dim(
        states, lax.axis_index("mp") * feature_count, feature_count, 1
    )
    residual = own_states + projected
    square_sum, head_sum = lax.psum(
        (jnp.sum(residual * residual, 1), jnp.sum(residual * value_weight[None, :], 1)), "mp"
    )
    value = head_sum * lax.rsqrt(square_sum / width + epsilon)
    following = from_behind(old_values[:1], "dp", -1)
    next_old = jnp.concatenate([old_values[1:], following])
    booted = jnp.where(finished > 0, (1.0 - stopped) * old_values, next_old)
    delta = rewards + discount * booted - old_values
    keep_rate = discount * trace_decay
    spacing = (order[None, :] - order[:, None]).astype(jnp.float32)
    forward_mask = (spacing >= 0.0) & same_episode
    decay_matrix = jnp.where(
        forward_mask, jnp.power(jnp.float32(keep_rate), jnp.maximum(spacing, 0.0)), 0.0
    )
    local_part = jnp.dot(decay_matrix, delta, precision=lax.Precision.HIGHEST)
    remaining = (rows - order).astype(jnp.float32)
    reach = jnp.where(episode == episode[-1], jnp.power(jnp.float32(keep_rate), remaining), 0.0) * (
        1.0 - finished[-1]
    )

    def compose(earlier, later_map):
        return (later_map[0] + later_map[1] * earlier[0], later_map[1] * earlier[1])

    prefix = carried_in(
        (local_part[:1], reach[:1]),
        "dp",
        compose,
        (jnp.zeros((1,), jnp.float32), jnp.ones((1,), jnp.float32)),
    )
    incoming = prefix[0][0]
    advantage = local_part + reach * incoming
    returns = advantage + old_values
    clipped = old_values + jnp.clip(value - old_values, -clip_range, clip_range)
    terms = jnp.maximum((value - returns) ** 2, (clipped - returns) ** 2)
    total_loss = lax.psum(jnp.sum(terms), "dp")
    value_loss = 0.5 * total_loss / (rows * lax.axis_size("dp"))
    return (value, advantage, value_loss)


def solution(mesh):
    return jax.shard_map(
        body,
        mesh=mesh,
        in_specs=(
            P("dp", None),
            P("dp", "mp"),
            P("dp", "mp"),
            P("dp", "mp"),
            P("dp", "mp"),
            P("mp"),
            P("dp"),
            P("dp"),
            P(),
            P(),
        ),
        out_specs=(P("dp"), P("dp"), P()),
        check_vma=False,
    )
```

profile of v0, /device:TPU:0, one launch (start us, length us, event | category | flops | bytes accessed | tf_op | source)
XLA Modules:
  0.0 487.3 jit_solution(12846572343256018310)
XLA Ops:
  7.2 0.7 all-gather.10.cloned.1.call-update
  7.9 0.7 all-gather.8.cloned.1.call-update
  8.7 0.7 all-gather.12.cloned.1.call-update
  9.4 0.5 all-gather.16.cloned.1.call-update
  10.0 0.0 all-gather.14.cloned.1.call-start
  10.0 0.7 copy.25
  10.8 0.1 reduce-window.7
  10.9 0.1 reduce
  11.0 0.8 fusion.22
  11.8 3.1 multiply_reduce_fusion
  14.9 0.2 compare_and_fusion.1
  15.1 1.0 multiply_cosine_fusion
  16.1 47.2 %all-gather.10.cloned.1.call-done = bf16[4096,512]{1,0:T(8,128)(2,1)} async-done(((bf16[256,512]{1,0:T(8,128)(2,1)}), bf16[4096,512]{1,0:T(8,128)(2,1)}) %all-gather.10.cloned.1.call-update) | async-done | bytes 4194320 | tf_op jit(solution)/shard_map/all_gather | solution.py:58
  63.3 5.9 %fusion.32 = f32[512,512]{0,1:T(8,128)S(1)} fusion(bf16[4096,512]{1,0:T(8,128)(2,1)} %all-gather.10.cloned.1.call-done, f32[512]{0:T(512)S(1)} %add_rsqrt_fusion, bf16[512,4096]{1,0:T(8,128)(2,1)} %param.12), kind=kOutput, calls=%fused_computation.70 | convolution fusion | flops 2153775104 | bytes 9439232 | tf_op jit(solution)/shard_map/dot_general | solution.py:64
  69.2 0.1 fusion.33
  69.3 0.3 copy.34
  69.6 0.3 copy.35
  69.9 1.1 subtract_convert_fusion.1
  71.0 43.3 %all-gather.8.cloned.1.call-done = bf16[4096,512]{1,0:T(8,128)(2,1)} async-done(((bf16[256,512]{1,0:T(8,128)(2,1)}), bf16[4096,512]{1,0:T(8,128)(2,1)}) %all-gather.8.cloned.1.call-update) | async-done | bytes 4194320 | tf_op jit(solution)/shard_map/all_gather | solution.py:59
  114.4 5.9 %convolution_convert_fusion = bf16[512,512]{0,1:T(8,128)(2,1)S(1)} fusion(bf16[4096,512]{1,0:T(8,128)(2,1)} %all-gather.8.cloned.1.call-done, f32[512]{0:T(512)S(1)} %add_rsqrt_fusion, bf16[512,4096]{1,0:T(8,128)(2,1)} %param.12), kind=kOutput, calls=%fused_computation.26 | convolution fusion | flops 2154037248 | bytes 8914944 | tf_op jit(solution)/shard_map/dot_general | solution.py:64
  120.3 121.2 %all-gather.12.cloned.1.call-done = bf16[4096,2048]{1,0:T(8,128)(2,1)} async-done(((bf16[256,2048]{1,0:T(8,128)(2,1)}), bf16[4096,2048]{1,0:T(8,128)(2,1)}) %all-gather.12.cloned.1.call-update) | async-done | bytes 16777232 | tf_op jit(solution)/shard_map/all_gather | solution.py:57
  241.5 13.2 %convolution_bitcast_fusion = f32[64,8,16,128]{3,1,2,0:T(8,128)S(1)} fusion(bf16[4096,2048]{1,0:T(8,128)(2,1)} %all-gather.12.cloned.1.call-done, f32[512]{0:T(512)S(1)} %add_rsqrt_fusion, bf16[512,4096]{1,0:T(8,128)(2,1)} %param.12), kind=kOutput, calls=%fused_computation.18 | convolution fusion | flops 8596226048 | bytes 25167872 | tf_op jit(solution)/shard_map/dot_general | solution.py:64
  254.8 0.9 copy.36
  255.7 1.8 subtract_convert_fusion
  257.5 0.5 copy.29
  258.1 0.5 copy.28
  258.6 8.1 %fusion.6 = f32[4,512,512,4]{2,1,3,0:T(8,128)} fusion(bf16[512,4,4,64]{3,0,2,1:T(8,128)(2,1)S(1)} %bitcast.53, bf16[512,4,4,64]{3,0,2,1:T(8,128)(2,1)S(1)} %bitcast.54, bf16[512,4,64]{2,0,1:T(8,128)(2,1)S(1)} %copy-done, bf16[512,4,64]{2,0,1:T(8,128)(2,1)S(1)} %get-tuple-element.113), kind=kOutput, calls=%fused_computation.19 | convolution fusion | flops 1078984704 | bytes 19398656 | tf_op jit(solution)/shard_map/tkgd,skd->kgts/dot_general | solution.py:84
  266.8 17.9 %fusion.34 = (f32[4,4,512]{2,1,0:T(4,128)S(1)}, f32[4,4,512,512]{2,3,1,0:T(8,128)}) fusion(f32[4,512,512,4]{2,1,3,0:T(8,128)} %fusion.6, pred[512,512]{0,1:T(8,128)(4,1)S(1)} %compare_and_fusion.1), kind=kOutput, calls=%fused_computation.72 | output fusion | flops 29360640 | bytes 33849344 | tf_op jit(solution)/shard_map/sub | solution.py:92
  284.7 8.6 %fusion.10 = bf16[4,128,4,512]{3,1,2,0:T(8,128)(2,1)} fusion(bf16[512,4,128,1]{0,2,3,1:T(8,128)(2,1)S(1)} %bitcast.63, f32[4,4,512,512]{2,3,1,0:T(8,128)} %get-tuple-element.120, f32[4,4,512]{2,1,0:T(4,128)S(1)} %get-tuple-element.119), kind=kOutput, calls=%fused_computation.23 | convolution fusion | flops 1083179008 | bytes 19431424 | tf_op jit(solution)/shard_map/kgts,skd->tkgd/dot_general | solution.py:94
  293.4 0.5 slice.35
  293.9 1.3 collective-permute-start
  295.2 6.5 %convert_element_type.45 = f32[512,4096]{1,0:T(8,128)} convert(bf16[512,4096]{1,0:T(8,128)(2,1)} %param.12) | non-fusion elementwise | flops 2097152 | bytes 12582912 | tf_op jit(solution)/shard_map/convert_element_type | solution.py:52
  301.7 0.6 slice.36
  302.4 0.1 slice.34
  302.4 0.1 compare_reduce_fusion
  302.5 0.6 slice.37
  303.8 0.6 dynamic-slice
  304.4 0.7 select_multiply_fusion
  305.1 0.7 slice_dynamic-update-slice_fusion
  305.8 0.7 fusion.25
  306.5 1.1 fusion.11
  307.6 0.7 slice_dynamic-update-slice_fusion.1
  308.3 34.8 %all-reduce.2 = (f32[16]{0:T(128)S(1)}, f32[16]{0:T(128)S(1)}) all-reduce(f32[16]{0:T(128)S(1)} %slice_dynamic-update-slice_fusion.1, f32[16]{0:T(128)S(1)} %slice_dynamic-update-slice_fusion), channel_id=2, replica_groups=mesh['dp'=16,'mp'=2] {'dp'}, use_global_device_ids=true, to_apply=%add | all-reduce | flops 32 | bytes 256
  343.1 28.6 %while.14 = (s32[]{:T(128)}, f32[1]{0:T(128)}, s32[]{:T(128)}, f32[16,1]{0,1:T(1,128)S(1)}, f32[16,1]{0,1:T(1,128)S(1)}, /*index=5*/s32[]{:T(128)}, s32[]{:T(128)}, s32[]{:T(128)}, s32[]{:T(128)}) while((s32[]{:T(128)}, f32[1]{0:T(128)}, s32[]{:T(128)}, f32[16,1]{0,1:T(1,128)S(1)}, f32[16,1]{0,1:T(1,128)S(1)}, /*index=5*/s32[]{:T(128)}, ...), condition=%wide.region_12.13_spmd, body=%wide.region_11.12_spmd.sunk | while | flops 8 | bytes 183 | solution.py:33
  343.1 0.6 constant_dynamic-slice_fusion.3
  345.0 0.6 constant_dynamic-slice_fusion.3
  346.9 0.6 constant_dynamic-slice_fusion.3
  348.9 0.6 constant_dynamic-slice_fusion.3
  350.8 0.6 constant_dynamic-slice_fusion.3
  352.7 0.6 constant_dynamic-slice_fusion.3
  354.6 0.6 constant_dynamic-slice_fusion.3
  356.5 0.6 constant_dynamic-slice_fusion.3
  358.4 0.6 constant_dynamic-slice_fusion.3
  360.3 0.6 constant_dynamic-slice_fusion.3
  362.2 0.6 constant_dynamic-slice_fusion.3
  364.1 0.6 constant_dynamic-slice_fusion.3
  366.0 0.6 constant_dynamic-slice_fusion.3
  367.9 0.6 constant_dynamic-slice_fusion.3
  369.8 0.6 constant_dynamic-slice_fusion.3
  371.7 53.4 %all-gather.14.cloned.1.call-done = bf16[512,4096]{0,1:T(8,128)(2,1)} async-done(((bf16[512,2048]{0,1:T(8,128)(2,1)}), bf16[512,4096]{0,1:T(8,128)(2,1)}) %all-gather.14.cloned.1.call-update) | async-done | bytes 4194320 | tf_op jit(solution)/shard_map/all_gather | solution.py:96
  425.1 14.6 %multiply_reduce_fusion.1 = (f32[512]{0:T(512)S(1)}, f32[512]{0:T(512)S(1)}) fusion(f32[2048]{0:T(1024)S(1)} %copy-done.3, bf16[512,4096]{0,1:T(8,128)(2,1)} %all-gather.14.cloned.1.call-done, bf16[4096,2048]{1,0:T(8,128)(2,1)} %all-gather.16.cloned.1.call-done, f32[512,4096]{1,0:T(8,128)} %convert_element_type.45, s32[]{:T(128)S(6)} %select_n.35), kind=kOutput, calls=%fused_computation.13 | convolution fusion | flops 8595177472 | bytes 25178116 | tf_op jit(solution)/shard_map/dot_general | solution.py:97
  439.7 4.9 %all-reduce.3 = (f32[512]{0:T(512)S(1)}, f32[512]{0:T(512)S(1)}) all-reduce(f32[512]{0:T(512)S(1)} %get-tuple-element.89, f32[512]{0:T(512)S(1)} %get-tuple-element.88), channel_id=1, replica_groups=mesh['dp'=16,'mp'=2] {'mp'}, use_global_device_ids=true, to_apply=%region_6.7 | all-reduce | flops 1024 | bytes 8192 | tf_op jit(solution)/shard_map/psum | solution.py:103
  444.7 1.9 maximum_reduce_fusion
  446.5 32.5 %psum.23 = f32[]{:T(128)} all-reduce(f32[]{:T(128)} %get-tuple-element.106), channel_id=1, replica_groups=mesh['dp'=16,'mp'=2] {'dp'}, use_global_device_ids=true, to_apply=%region_14.15 | all-reduce | flops 1 | bytes 8 | tf_op jit(solution)/shard_map/psum | solution.py:137
  (25 shorter events, 0.3 us)
Async XLA Ops:
  7.2 56.1 %all-gather.10.cloned.1.call-start = ((), (), s32[]{:S(2)}) async-start(), calls=%async_computation.1 | async-start | bytes 4456448 | tf_op jit(solution)/shard_map/all_gather | solution.py:58
  7.9 106.5 %all-gather.8.cloned.1.call-start = ((), (), s32[]{:S(2)}) async-start(), calls=%async_computation | async-start | bytes 4456448 | tf_op jit(solution)/shard_map/all_gather | solution.py:59
  8.7 232.9 %all-gather.12.cloned.1.call-start = ((), (), s32[]{:S(2)}) async-start(), calls=%async_computation.2 | async-start | bytes 17825792 | tf_op jit(solution)/shard_map/all_gather | solution.py:57
  9.4 362.3 %all-gather.16.cloned.1.call-start = ((), (), s32[]{:S(2)}) async-start(), calls=%async_computation.4 | async-start | bytes 17825792 | tf_op jit(solution)/shard_map/all_gather | solution.py:60
  10.0 415.2 %all-gather.14.cloned.1.call-start = ((), (), s32[]{:S(2)}) async-start(), calls=%async_computation.3 | async-start | bytes 6291456 | tf_op jit(solution)/shard_map/all_gather | solution.py:96
  257.5 1.1 copy-start
  284.7 8.6 %copy-start.1 = (f32[512]{0:T(512)S(1)}, f32[512]{0:T(512)}, u32[]{:S(2)}) copy-start(f32[512]{0:T(512)} %param.19) | copy-start | bytes 6148
  293.9 12.0 %collective-permute-start = (f32[1]{0:T(128)}, f32[1]{0:T(128)}, u32[]{:S(2)}, u32[]{:S(2)}) collective-permute-start(f32[1]{0:T(128)} %slice.35), channel_id=1, source_target_pairs={{2,0},{4,2},{6,4},{8,6},{10,8},{12,10},{14,12},{16,14},{18,16},{20... | collective-permute-start | bytes 20 | tf_op jit(solution)/shard_map/ppermute | solution.py:17
  295.2 8.6 %copy-start.4 = (u32[32]{0:T(128)S(1)}, u32[32]{0:T(128)}, u32[]{:S(2)}) copy-start(u32[32]{0:T(128)} %constant.106) | copy-start | bytes 388
  295.2 10.7 %copy-start.2 = (f32[512]{0:T(512)S(1)}, f32[512]{0:T(512)}, u32[]{:S(2)}) copy-start(f32[512]{0:T(512)} %param.18) | copy-start | bytes 6148
  295.2 130.0 %copy-start.3 = (f32[2048]{0:T(1024)S(1)}, f32[2048]{0:T(1024)}, u32[]{:S(2)}) copy-start(f32[2048]{0:T(1024)} %param.17) | copy-start | bytes 24580
Sparse Core Ops, SparseCore 0:
  10.1 53.0 all-gather.9
  65.4 48.8 all-gather.7
  116.5 124.9 all-gather.11
  243.6 125.2 all-gather.15
  370.2 54.8 all-gather.13
where the time goes:
time: 488 us; the launch traced here: 487 us
  waiting for transfers between devices  268 us (55%)
  blocking collectives  72.2 us (15%)
  matrix products  57.5 us (12%)
  other arithmetic  36 us (7%)
  loops' own time  19.3 us (4%)
  local copies, waits for them, and re-layouts  16.7 us (3%)
  between operations  16.4 us (3%)
    all_gather x1, waiting for transfers between devices, body(): lax.all_gather(w_query, 'dp', axis=0, tiled=True)  121 us
    all_gather x1, waiting for transfers between devices, body(): all_heads = lax.all_gather(attended, 'mp', axis=1, tiled=True)  53.4 us
    all_gather x1, waiting for transfers between devices, body(): lax.all_gather(w_key, 'dp', axis=0, tiled=True)  47.2 us
    all_gather x1, waiting for transfers between devices, body(): lax.all_gather(w_value, 'dp', axis=0, tiled=True)  43.3 us
    unnamed x1, blocking collectives  34.8 us
    psum x1, blocking collectives, body(): total_loss = lax.psum(jnp.sum(terms), 'dp')  32.5 us
    dot_general x3, matrix products, body(): jnp.dot(normed, piece, preferred_element_type=jnp.float32)  25 us
    another operation x1, loops' own time, carried_in(): return lax.fori_loop(0, ahead, one, state)  19.3 us
  transfers between devices with their start and end apart: 6, of which 4 were waited for; matrix products, arithmetic and copies ran while one was open for 19% of the time, Pallas kernels for 0%

commit v1 on v0

--- a/solution.py
+++ b/solution.py
@@ -93,7 +93,15 @@
     probs = (expon / jnp.sum(expon, -1, keepdims=True)).astype(jnp.bfloat16)
     output = jnp.einsum("kgts,skd->tkgd", probs, values_proj, preferred_element_type=jnp.float32)
     attended = output.astype(jnp.bfloat16).reshape(rows, local_heads * HEAD)
-    all_heads = lax.all_gather(attended, "mp", axis=1, tiled=True)
+    ways, here = (lax.axis_size("mp"), lax.axis_index("mp"))
+    grown, reach_2 = (attended, 1)
+    while reach_2 < ways:
+        theirs = lax.ppermute(grown, "mp", [(d, d ^ reach_2) for d in range(ways)])
+        mine_first = jnp.concatenate([grown, theirs], axis=1)
+        theirs_first = jnp.concatenate([theirs, grown], axis=1)
+        grown = jnp.where(here & reach_2 == 0, mine_first, theirs_first)
+        reach_2 = 2 * reach_2
+    all_heads = grown
     projected = jnp.dot(all_heads, whole_out, preferred_element_type=jnp.float32)
     feature_count = w_out.shape[1]
     own_states = lax.dynamic_slice_in_dim(

time: 488 us -> 437 us (0.90)
  waiting for transfers between devices: 268 us -> 214 us
    all_gather x1 -> x0, waiting for transfers between devices: 53.4 us -> none  [body(): all_heads = lax.all_gather(attended, 'mp', axis=1, tiled=True)]
  transfers between devices with their start and end apart: 6 -> 6, of which waited for: 4 -> 3; matrix products, arithmetic and copies ran while one was open for 19% -> 21% of each run, Pallas kernels for 0% -> 0%
where the time goes in v1:
time: 437 us; the launch traced here: 436 us
  waiting for transfers between devices  214 us (49%)
  blocking collectives  70.1 us (16%)
  matrix products  59 us (14%)
  other arithmetic  35.6 us (8%)
  loops' own time  20.2 us (5%)
  local copies, waits for them, and re-layouts  17.2 us (4%)
  between operations  16.4 us (4%)
    all_gather x1, waiting for transfers between devices, body(): lax.all_gather(w_query, 'dp', axis=0, tiled=True)  121 us
    all_gather x1, waiting for transfers between devices, body(): lax.all_gather(w_key, 'dp', axis=0, tiled=True)  47.2 us
    all_gather x1, waiting for transfers between devices, body(): lax.all_gather(w_value, 'dp', axis=0, tiled=True)  43.3 us
    unnamed x1, blocking collectives  35.1 us
    psum x1, blocking collectives, body(): total_loss = lax.psum(jnp.sum(terms), 'dp')  30.1 us
    dot_general x3, matrix products, body(): jnp.dot(normed, piece, preferred_element_type=jnp.float32)  25 us
    another operation x1, loops' own time, carried_in(): return lax.fori_loop(0, ahead, one, state)  20.2 us
    sub x1, other arithmetic, body(): expon = jnp.where(allowed[None, None], jnp.exp(masked - largest), 0.0)  17.9 us
  transfers between devices with their start and end apart: 6, of which 3 were waited for; matrix products, arithmetic and copies ran while one was open for 21% of the time, Pallas kernels for 0%

profile of v1, /device:TPU:0, one launch (start us, length us, event | category | flops | bytes accessed | tf_op | source)
XLA Modules:
  0.0 435.9 jit_solution(8704063032176392789)
XLA Ops:
  7.2 0.7 all-gather.9.cloned.1.call-update
  7.9 0.7 all-gather.7.cloned.1.call-update
  8.7 0.7 all-gather.11.cloned.1.call-update
  9.4 0.0 all-gather.13.cloned.1.call-start
  9.4 0.5 all-gather.13.cloned.1.call-update
  10.0 0.7 copy.25
  10.7 0.1 reduce-window.7
  10.8 0.1 reduce
  11.0 0.8 fusion.29
  11.7 3.1 multiply_reduce_fusion
  14.8 0.2 compare_and_fusion.1
  15.1 1.0 multiply_cosine_fusion
  16.0 47.2 %all-gather.9.cloned.1.call-done = bf16[4096,512]{1,0:T(8,128)(2,1)} async-done(((bf16[256,512]{1,0:T(8,128)(2,1)}), bf16[4096,512]{1,0:T(8,128)(2,1)}) %all-gather.9.cloned.1.call-update) | async-done | bytes 4194320 | tf_op jit(solution)/shard_map/all_gather | solution.py:58
  63.3 5.9 %fusion.40 = f32[512,512]{0,1:T(8,128)S(1)} fusion(bf16[4096,512]{1,0:T(8,128)(2,1)} %all-gather.9.cloned.1.call-done, f32[512]{0:T(512)S(1)} %add_rsqrt_fusion, bf16[512,4096]{1,0:T(8,128)(2,1)} %param.12), kind=kOutput, calls=%fused_computation.79 | convolution fusion | flops 2153775104 | bytes 9439232 | tf_op jit(solution)/shard_map/dot_general | solution.py:64
  69.2 0.1 fusion.41
  69.3 0.3 copy.34
  69.6 0.3 copy.35
  70.0 1.1 subtract_convert_fusion.1
  71.0 43.3 %all-gather.7.cloned.1.call-done = bf16[4096,512]{1,0:T(8,128)(2,1)} async-done(((bf16[256,512]{1,0:T(8,128)(2,1)}), bf16[4096,512]{1,0:T(8,128)(2,1)}) %all-gather.7.cloned.1.call-update) | async-done | bytes 4194320 | tf_op jit(solution)/shard_map/all_gather | solution.py:59
  114.4 5.9 %convolution_convert_fusion = bf16[512,512]{0,1:T(8,128)(2,1)S(1)} fusion(bf16[4096,512]{1,0:T(8,128)(2,1)} %all-gather.7.cloned.1.call-done, f32[512]{0:T(512)S(1)} %add_rsqrt_fusion, bf16[512,4096]{1,0:T(8,128)(2,1)} %param.12), kind=kOutput, calls=%fused_computation.34 | convolution fusion | flops 2154037248 | bytes 8914944 | tf_op jit(solution)/shard_map/dot_general | solution.py:64
  120.3 121.2 %all-gather.11.cloned.1.call-done = bf16[4096,2048]{1,0:T(8,128)(2,1)} async-done(((bf16[256,2048]{1,0:T(8,128)(2,1)}), bf16[4096,2048]{1,0:T(8,128)(2,1)}) %all-gather.11.cloned.1.call-update) | async-done | bytes 16777232 | tf_op jit(solution)/shard_map/all_gather | solution.py:57
  241.5 13.2 %convolution_bitcast_fusion = f32[64,8,16,128]{3,1,2,0:T(8,128)S(1)} fusion(bf16[4096,2048]{1,0:T(8,128)(2,1)} %all-gather.11.cloned.1.call-done, f32[512]{0:T(512)S(1)} %add_rsqrt_fusion, bf16[512,4096]{1,0:T(8,128)(2,1)} %param.12), kind=kOutput, calls=%fused_computation.26 | convolution fusion | flops 8596226048 | bytes 25167872 | tf_op jit(solution)/shard_map/dot_general | solution.py:64
  254.7 0.9 copy.36
  255.7 1.7 subtract_convert_fusion
  257.4 0.5 copy.29
  257.9 0.5 copy.28
  258.5 8.1 %fusion.13 = f32[4,512,512,4]{2,1,3,0:T(8,128)} fusion(bf16[512,4,4,64]{3,0,2,1:T(8,128)(2,1)S(1)} %bitcast.52, bf16[512,4,4,64]{3,0,2,1:T(8,128)(2,1)S(1)} %bitcast.53, bf16[512,4,64]{2,0,1:T(8,128)(2,1)S(1)} %copy-done, bf16[512,4,64]{2,0,1:T(8,128)(2,1)S(1)} %get-tuple-element.113), kind=kOutput, calls=%fused_computation.27 | convolution fusion | flops 1078984704 | bytes 19398656 | tf_op jit(solution)/shard_map/tkgd,skd->kgts/dot_general | solution.py:84
  266.6 17.9 %fusion.42 = (f32[4,4,512]{2,1,0:T(4,128)S(1)}, f32[4,4,512,512]{2,3,1,0:T(8,128)}) fusion(f32[4,512,512,4]{2,1,3,0:T(8,128)} %fusion.13, pred[512,512]{0,1:T(8,128)(4,1)S(1)} %compare_and_fusion.1), kind=kOutput, calls=%fused_computation.81 | output fusion | flops 29360640 | bytes 33849344 | tf_op jit(solution)/shard_map/sub | solution.py:92
  284.5 7.1 %fusion.17 = bf16[4,128,4,512]{3,1,2,0:T(8,128)(2,1)S(1)} fusion(bf16[512,4,128,1]{0,2,3,1:T(8,128)(2,1)S(1)} %bitcast.63, f32[4,4,512,512]{2,3,1,0:T(8,128)} %get-tuple-element.120, f32[4,4,512]{2,1,0:T(4,128)S(1)} %get-tuple-element.119), kind=kOutput, calls=%fused_computation.31 | convolution fusion | flops 1083179008 | bytes 19431424 | tf_op jit(solution)/shard_map/kgts,skd->tkgd/dot_general | solution.py:94
  291.6 1.5 collective-permute-start
  293.1 0.5 slice.35
  293.6 1.3 collective-permute-start.1
  294.9 6.5 %convert_element_type.45 = f32[512,4096]{1,0:T(8,128)} convert(bf16[512,4096]{1,0:T(8,128)(2,1)} %param.12) | non-fusion elementwise | flops 2097152 | bytes 12582912 | tf_op jit(solution)/shard_map/convert_element_type | solution.py:52
  301.4 0.6 slice.36
  302.0 0.1 slice.34
  302.1 0.1 compare_reduce_fusion
  302.2 0.6 slice.37
  303.3 0.6 dynamic-slice
  304.0 0.6 select_multiply_fusion
  304.5 0.8 slice_dynamic-update-slice_fusion
  305.3 0.8 fusion.32
  306.1 1.1 fusion.18
  307.2 0.8 slice_dynamic-update-slice_fusion.1
  307.9 35.1 %all-reduce.2 = (f32[16]{0:T(128)S(1)}, f32[16]{0:T(128)S(1)}) all-reduce(f32[16]{0:T(128)S(1)} %slice_dynamic-update-slice_fusion.1, f32[16]{0:T(128)S(1)} %slice_dynamic-update-slice_fusion), channel_id=2, replica_groups=mesh['dp'=16,'mp'=2] {'dp'}, use_global_device_ids=true, to_apply=%add | all-reduce | flops 32 | bytes 256
  343.0 30.0 %while.14 = (s32[]{:T(128)}, f32[1]{0:T(128)}, s32[]{:T(128)}, f32[16,1]{0,1:T(1,128)S(1)}, f32[16,1]{0,1:T(1,128)S(1)}, /*index=5*/s32[]{:T(128)}, s32[]{:T(128)}, s32[]{:T(128)}, s32[]{:T(128)}) while((s32[]{:T(128)}, f32[1]{0:T(128)}, s32[]{:T(128)}, f32[16,1]{0,1:T(1,128)S(1)}, f32[16,1]{0,1:T(1,128)S(1)}, /*index=5*/s32[]{:T(128)}, ...), condition=%wide.region_12.13_spmd, body=%wide.region_11.12_spmd.sunk | while | flops 8 | bytes 183 | solution.py:33
  343.1 0.7 constant_dynamic-slice_fusion.3
  345.1 0.7 constant_dynamic-slice_fusion.3
  347.1 0.7 constant_dynamic-slice_fusion.3
  349.1 0.7 constant_dynamic-slice_fusion.3
  351.1 0.7 constant_dynamic-slice_fusion.3
  353.1 0.7 constant_dynamic-slice_fusion.3
  355.1 0.7 constant_dynamic-slice_fusion.3
  357.1 0.7 constant_dynamic-slice_fusion.3
  359.1 0.7 constant_dynamic-slice_fusion.3
  361.1 0.7 constant_dynamic-slice_fusion.3
  363.1 0.7 constant_dynamic-slice_fusion.3
  365.1 0.7 constant_dynamic-slice_fusion.3
  367.1 0.7 constant_dynamic-slice_fusion.3
  369.1 0.7 constant_dynamic-slice_fusion.3
  371.1 0.7 constant_dynamic-slice_fusion.3
  373.1 17.6 %multiply_reduce_fusion.1 = (f32[512]{0:T(512)S(1)}, f32[512]{0:T(512)S(1)}) fusion(f32[2048]{0:T(1024)S(1)} %copy-done.3, bf16[4096,2048]{1,0:T(8,128)(2,1)} %all-gather.13.cloned.1.call-done, bf16[512,2048]{0,1:T(8,128)(2,1)} %collective-permute-done, bf16[512,2048]{0,1:T(8,128)(2,1)S(1)} %bitcast.62, pred[]{:T(512)S(6)} %eq.37, ...), kind=kOutput, calls=%fused_computation.20 | convolution fusion | flops 8614051840 | bytes 25178116 | tf_op jit(solution)/shard_map/dot_general | solution.py:105
  390.8 4.9 %all-reduce.3 = (f32[512]{0:T(512)S(1)}, f32[512]{0:T(512)S(1)}) all-reduce(f32[512]{0:T(512)S(1)} %get-tuple-element.89, f32[512]{0:T(512)S(1)} %get-tuple-element.88), channel_id=1, replica_groups=mesh['dp'=16,'mp'=2] {'mp'}, use_global_device_ids=true, to_apply=%region_6.7 | all-reduce | flops 1024 | bytes 8192 | tf_op jit(solution)/shard_map/psum | solution.py:111
  395.7 1.7 maximum_reduce_fusion
  397.5 30.1 %psum.23 = f32[]{:T(128)} all-reduce(f32[]{:T(128)} %get-tuple-element.106), channel_id=1, replica_groups=mesh['dp'=16,'mp'=2] {'dp'}, use_global_device_ids=true, to_apply=%region_14.15 | all-reduce | flops 1 | bytes 8 | tf_op jit(solution)/shard_map/psum | solution.py:145
  (24 shorter events, 0.2 us)
Async XLA Ops:
  7.2 56.1 %all-gather.9.cloned.1.call-start = ((), (), s32[]{:S(2)}) async-start(), calls=%async_computation.1 | async-start | bytes 4456448 | tf_op jit(solution)/shard_map/all_gather | solution.py:58
  7.9 106.5 %all-gather.7.cloned.1.call-start = ((), (), s32[]{:S(2)}) async-start(), calls=%async_computation | async-start | bytes 4456448 | tf_op jit(solution)/shard_map/all_gather | solution.py:59
  8.7 232.9 %all-gather.11.cloned.1.call-start = ((), (), s32[]{:S(2)}) async-start(), calls=%async_computation.2 | async-start | bytes 17825792 | tf_op jit(solution)/shard_map/all_gather | solution.py:57
  9.4 363.7 %all-gather.13.cloned.1.call-start = ((), (), s32[]{:S(2)}) async-start(), calls=%async_computation.3 | async-start | bytes 17825792 | tf_op jit(solution)/shard_map/all_gather | solution.py:60
  257.4 1.1 copy-start
  284.5 8.5 %copy-start.1 = (f32[512]{0:T(512)S(1)}, f32[512]{0:T(512)}, u32[]{:S(2)}) copy-start(f32[512]{0:T(512)} %param.19) | copy-start | bytes 6148
  291.6 81.5 %collective-permute-start = (bf16[512,2048]{0,1:T(8,128)(2,1)S(1)}, bf16[512,2048]{0,1:T(8,128)(2,1)}, u32[]{:S(2)}, u32[]{:S(2)}) collective-permute-start(bf16[512,2048]{0,1:T(8,128)(2,1)S(1)} %bitcast.61), channel_id=1, source_target_pairs={{0,1},{1,0},{2,3},{3,2},{4,5},{5,4},{6,7},{7,6},{8,9},{9,8},{10,11... | collective-permute-start | bytes 6291464 | tf_op jit(solution)/shard_map/ppermute | solution.py:99
  293.6 11.7 %collective-permute-start.1 = (f32[1]{0:T(128)}, f32[1]{0:T(128)}, u32[]{:S(2)}, u32[]{:S(2)}) collective-permute-start(f32[1]{0:T(128)} %slice.35), channel_id=1, source_target_pairs={{2,0},{4,2},{6,4},{8,6},{10,8},{12,10},{14,12},{16,14},{18,16},{20... | collective-permute-start | bytes 20 | tf_op jit(solution)/shard_map/ppermute | solution.py:17
  294.9 8.4 %copy-start.4 = (u32[32]{0:T(128)S(1)}, u32[32]{0:T(128)}, u32[]{:S(2)}) copy-start(u32[32]{0:T(128)} %constant.108) | copy-start | bytes 388
  294.9 10.4 %copy-start.2 = (f32[512]{0:T(512)S(1)}, f32[512]{0:T(512)}, u32[]{:S(2)}) copy-start(f32[512]{0:T(512)} %param.18) | copy-start | bytes 6148
  294.9 78.2 %copy-start.3 = (f32[2048]{0:T(1024)S(1)}, f32[2048]{0:T(1024)}, u32[]{:S(2)}) copy-start(f32[2048]{0:T(1024)} %param.17) | copy-start | bytes 24580
Sparse Core Ops, SparseCore 0:
  10.1 53.0 all-gather.8
  65.4 48.8 all-gather.6
  116.5 124.9 all-gather.10
  243.6 125.2 all-gather.12
